TPU v7x, 128 devices: a whole 4x4x4 slice. The times are simulated.
128 devices in a mesh: freq: 4 (over z_hi, core), pos: 32 (over x, y, z_lo).
Axes of the slice: x: 4, y: 4, z: 4 (z_hi: 2, z_lo: 2; z = z_hi * 2 + z_lo), core: 2. Of those that a mesh axis runs over, the one named last changes fastest.
Arguments:
- spectra: bfloat16 [16, 2, 256, 32768], P(None, None, 'freq', 'pos'), may hold values from -6 to 6
- green: bfloat16 [16, 32768, 2048], P('freq', 'pos'), may hold values from -0.0234375 to 0.0234375
- recorded: bfloat16 [256, 1024, 512], P('pos', 'freq'), may hold values from -6 to 6
- filter_taps: float32 [256, 11], P('pos'), may hold values from -3 to 3
Outputs:
- primaries: bfloat16 [256, 1024, 512], P('pos', 'freq')
All inputs are finite; a program needn't handle non-finite values.
Results may differ from a plain program's by a relative error of at most 0.001.
Values may be sent and summed in bfloat16 or wider, within the bound.
No kernel may reach another device: no remote copies, remote signals or barrier semaphores. Data moves between devices by JAX's collectives and lax.ppermute only.
A program may use at most 128 MiB of HBM per device.

v0:
```python
import jax
import jax.numpy as jnp
from jax import lax
from jax.sharding import Mesh
from jax.sharding import PartitionSpec as P

BAND_START = 32
FREQ = ("freq_0", "freq_1")
POS = ("pos_0", "pos_1", "pos_2")


def sum_by_axis(subtotal, axes):
    for axis in axes:
        subtotal = lax.psum_scatter(subtotal, axis, scatter_dimension=0, tiled=True)
    return subtotal


def cut_along(array, dim, devices):
    before, after = (array.shape[:dim], array.shape[dim + 1 :])
    return jnp.moveaxis(array.reshape(*before, devices, -1, *after), dim, 0)


def joined_along(parts, dim):
    shape = list(parts.shape[1:])
    shape[dim] *= parts.shape[0]
    return jnp.moveaxis(parts, 0, dim).reshape(shape)


def moved_by_axis(parts, axes, order):
    shape = [lax.axis_size(a) for a in axes]
    parts = parts.reshape(*shape, *parts.shape[1:])
    for k in order:
        parts = lax.all_to_all(parts, axes[k], split_axis=k, concat_axis=k, tiled=True)
    return parts.reshape(-1, *parts.shape[len(axes) :])


def core_and_chips(array, groups, order, split_dim, concat_dim):
    devices = lax.axis_size(groups[0]) * lax.axis_size(groups[1])
    parts = cut_along(array, split_dim, devices)
    return joined_along(moved_by_axis(parts, groups, order), concat_dim)


def phase_table(first_freq, freq_count, total_freqs, samples):
    bins = BAND_START + first_freq + jnp.arange(freq_count, dtype=jnp.int32)
    sample_index = jnp.arange(samples, dtype=jnp.int32)
    phase = bins[:, None] * sample_index[None, :] % samples
    angle = 2.0 * jnp.pi / samples * phase.astype(jnp.float32)
    scale = 1.0 / jnp.sqrt(jnp.float32(total_freqs))
    return jnp.stack([jnp.cos(angle), -jnp.sin(angle)], 1) * scale


def on_device(spectra, green, recorded, filter_taps):
    regrouped = lax.all_to_all(spectra, FREQ, split_axis=0, concat_axis=2, tiled=True)
    half_cols = green.shape[2] // 2
    product = jnp.einsum("fisk,fkr->sfir", regrouped, green, preferred_element_type=jnp.float32)
    real_part = product[:, :, 0, :half_cols] - product[:, :, 1, half_cols:]
    imag_part = product[:, :, 0, half_cols:] + product[:, :, 1, :half_cols]
    own_share = sum_by_axis(jnp.stack([real_part, imag_part], 2), POS)
    samples = recorded.shape[2]
    total_freqs = spectra.shape[0]
    spread = core_and_chips(own_share, ("freq_0", "freq_1"), (1, 0), 3, 1)
    table = phase_table(0, total_freqs, total_freqs, samples)
    traces = jnp.einsum("sfir,fit->srt", spread, table, precision=lax.Precision.HIGHEST)
    tap_count = filter_taps.shape[1]
    margin = (tap_count - 1) // 2
    padded = jnp.pad(traces, ((0, 0), (0, 0), (margin, margin)))
    result = recorded.astype(jnp.float32)
    for lag in range(tap_count):
        result = result - filter_taps[:, lag][:, None, None] * padded[:, :, lag : lag + samples]
    return result.astype(jnp.bfloat16)


def solution(mesh):
    torus = Mesh(
        mesh.devices.reshape(2, 2, 4, 4, 2), ("freq_0", "freq_1", "pos_0", "pos_1", "pos_2")
    )
    placed = (P(None, None, FREQ, POS), P(FREQ, POS, None), P(POS, FREQ, None), P(POS, None))
    return jax.shard_map(
        on_device, mesh=torus, in_specs=placed, out_specs=P(POS, FREQ, None), check_vma=False
    )
```

profile of v0, /device:TPU:0, one launch (start us, length us, event | category | flops | bytes accessed | tf_op | source)
XLA Modules:
  0.0 406.5 jit_solution(1218572337466034315)
XLA Ops:
  6.5 54.9 %all_to_all.28 = bf16[16,2,64,1024]{3,2,1,0:T(8,128)(2,1)S(1)} all-to-all(bf16[16,2,64,1024]{3,2,1,0:T(8,128)(2,1)} %param.4), channel_id=1, replica_groups=mesh['freq_0'=2,'freq_1'=2,'pos_0'=4,'pos_1'=4,'pos_2'=2] {'freq_0','fre..., dimensions={0} | all-to-all | bytes 8388608 | tf_op jit(solution)/shard_map/all_to_all | solution.py:53
  61.4 2.4 copy.19
  63.8 18.0 %fusion.2 = f32[256,4,2,2048]{0,3,2,1:T(8,128)} fusion(bf16[4,2,256,1024]{3,2,1,0:T(8,128)(2,1)} %bitcast.36, bf16[4,1024,2048]{2,1,0:T(8,128)(2,1)} %param.5), kind=kOutput, calls=%fused_computation.13 | convolution fusion | flops 8589934592 | bytes 37748736 | tf_op jit(solution)/shard_map/fisk,fkr->sfir/dot_general | solution.py:55
  81.8 9.2 %slice_subtract_fusion = (f32[256,4,1,1024]{0,3,2,1:T(8,128)S(1)}, f32[256,4,1,1024]{0,3,2,1:T(8,128)}) fusion(f32[256,4,2,2048]{0,3,2,1:T(8,128)} %fusion.2), kind=kLoop, calls=%fused_computation.36 | loop fusion | flops 2097152 | bytes 25165824 | tf_op jit(solution)/shard_map/sub | solution.py:56
  91.0 6.1 %pad_maximum_fusion = f32[256,4,2,1024]{0,3,2,1:T(8,128)} fusion(f32[256,4,1,1024]{0,3,2,1:T(8,128)} %get-tuple-element.17, f32[256,4,1,1024]{0,3,2,1:T(8,128)S(1)} %get-tuple-element.16), kind=kLoop, calls=%fused_computation.2 | loop fusion | flops 2097152 | bytes 16777216 | tf_op jit(solution)/shard_map/stack | solution.py:58
  97.1 10.5 %copy.21 = f32[256,4,2,1024]{3,1,2,0:T(4,128)} copy(f32[256,4,2,1024]{0,3,2,1:T(8,128)} %pad_maximum_fusion) | data formatting | bytes 16777216 | tf_op jit(solution)/shard_map/stack | solution.py:58
  107.6 0.0 all-reduce.8.cloned.1.call-update
  107.7 0.0 all-reduce.10.cloned.1.call-start
  107.7 0.5 copy-done.4
  108.3 0.6 dynamic-slice
  109.5 157.7 %all-reduce.8.cloned.1.call-done = f32[256,4,2,1024]{3,1,2,0:T(4,128)} async-done(((f32[256,4,2,1024]{3,1,2,0:T(4,128)}), f32[256,4,2,1024]{3,1,2,0:T(4,128)}) %all-reduce.8.cloned.1.call-update) | async-done | bytes 8388624
  267.2 3.2 constant_dynamic-slice_fusion.2
  270.4 0.0 all-reduce.10.cloned.1.call-update
  270.5 0.0 all-reduce.12.cloned.1.call-start
  270.5 0.6 dynamic-slice.2
  271.7 57.4 %all-reduce.10.cloned.1.call-done = f32[64,4,2,1024]{3,1,2,0:T(4,128)} async-done(((f32[64,4,2,1024]{3,1,2,0:T(4,128)}), f32[64,4,2,1024]{3,1,2,0:T(4,128)}) %all-reduce.10.cloned.1.call-update) | async-done | bytes 2097168
  329.2 1.9 constant_dynamic-slice_fusion.1
  331.1 0.7 dynamic-slice.4
  332.5 34.4 %all-reduce.12.cloned.1.call-done = f32[16,4,2,1024]{3,1,2,0:T(4,128)} async-done(((f32[16,4,2,1024]{3,1,2,0:T(4,128)}), f32[16,4,2,1024]{3,1,2,0:T(4,128)}) %all-reduce.12.cloned.1.call-update) | async-done | bytes 524304
  366.8 1.0 constant_dynamic-slice_fusion
  367.8 0.2 reshape.130
  368.0 0.2 copy.23
  368.2 4.1 %all_to_all.29 = f32[2,2,8,4,2,256]{5,2,4,3,0,1:T(8,128)S(1)} all-to-all(f32[2,2,8,4,2,256]{5,2,4,3,0,1:T(8,128)S(1)} %copy.24), channel_id=1, replica_groups=mesh['freq_0'=2,'freq_1'=2,'pos_0'=4,'pos_1'=4,'pos_2'=2] {'freq_1'}, dimensions={1} | all-to-all | bytes 524288 | tf_op jit(solution)/shard_map/all_to_all | solution.py:33
  372.3 0.7 copy.25
  373.0 4.1 %all-to-all-start.2 = ((f32[2,2,8,4,2,256]{5,2,4,3,1,0:T(8,128)}), f32[2,2,8,4,2,256]{5,2,4,3,1,0:T(8,128)S(1)}, u32[]{:S(2)}, u32[]{:S(2)}) async-start(f32[2,2,8,4,2,256]{5,2,4,3,1,0:T(8,128)} %copy.25), calls=%async_computation.2 | async-start | bytes 524288 | tf_op jit(solution)/shard_map/all_to_all | solution.py:33
  377.1 0.2 fusion.38
  377.3 0.3 slice_reduce_fusion.10
  377.7 6.4 %all-to-all-done.2 = f32[2,2,8,4,2,256]{5,2,4,3,1,0:T(8,128)S(1)} async-done(((f32[2,2,8,4,2,256]{5,2,4,3,1,0:T(8,128)}), f32[2,2,8,4,2,256]{5,2,4,3,1,0:T(8,128)S(1)}, u32[]{:S(2)}, u32[]{:S(2)}) %all-to-all-start.2) | async-done | bytes 262176 | tf_op jit(solution)/shard_map/all_to_all | solution.py:33
  384.1 0.2 copy.34
  384.3 0.1 reshape.126
  384.4 3.5 convolution_bitcast_fusion
  387.9 12.1 %fusion.26 = bf16[8,256,512]{2,1,0:T(8,128)(2,1)} fusion(f32[8,256,512]{2,1,0:T(8,128)S(1)} %convolution_bitcast_fusion, bf16[8,256,512]{2,1,0:T(8,128)(2,1)S(1)} %copy-done, f32[8]{0:T(128)S(1)} %get-tuple-element.14, f32[8]{0:T(128)S(1)} %get-tuple-element.15, f32[8]{0:T(128)S(1)} %get-tuple-element.6, f32[8]{0:T(128)S(1)} %get-tuple-element.7, ...), kind=kLoop, calls=%fused_computation.37 | loop fusion | flops 25165824 | bytes 8388960 | tf_op jit(solution)/shard_map/convert_element_type | solution.py:70
  (13 shorter events, 0.1 us)
Async XLA Ops:
  6.5 260.7 %all-reduce.8.cloned.1.call-start = ((), (), s32[]{:S(2)}) async-start(), calls=%async_computation.3 | async-start | bytes 16777216
  107.6 0.7 copy-start.4
  107.6 162.9 %copy-start.3 = (u32[128]{0:T(128)S(1)}, u32[128]{0:T(128)}, u32[]{:S(2)}) copy-start(u32[128]{0:T(128)} %constant.34) | copy-start | bytes 1540
  107.6 223.4 %copy-start.2 = (u32[128]{0:T(128)S(1)}, u32[128]{0:T(128)}, u32[]{:S(2)}) copy-start(u32[128]{0:T(128)} %constant.38) | copy-start | bytes 1540
  107.7 221.5 %all-reduce.10.cloned.1.call-start = ((), (), s32[]{:S(2)}) async-start(), calls=%async_computation.4 | async-start | bytes 4194304
  270.4 106.9 %copy-start.1 = (f32[8,11]{1,0:T(8,128)S(1)}, f32[8,11]{1,0:T(8,128)}, u32[]{:S(2)}) copy-start(f32[8,11]{1,0:T(8,128)} %param.7) | copy-start | bytes 1060
  270.5 96.4 %all-reduce.12.cloned.1.call-start = ((), (), s32[]{:S(2)}) async-start(), calls=%async_computation.5 | async-start | bytes 1048576
  368.0 19.9 %copy-start = (bf16[8,256,512]{2,1,0:T(8,128)(2,1)S(1)}, bf16[8,256,512]{2,1,0:T(8,128)(2,1)}, u32[]{:S(2)}) copy-start(bf16[8,256,512]{2,1,0:T(8,128)(2,1)} %param.6) | copy-start | bytes 6291460
  373.0 11.1 %all-to-all-start.2 = ((f32[2,2,8,4,2,256]{5,2,4,3,1,0:T(8,128)}), f32[2,2,8,4,2,256]{5,2,4,3,1,0:T(8,128)S(1)}, u32[]{:S(2)}, u32[]{:S(2)}) async-start(f32[2,2,8,4,2,256]{5,2,4,3,1,0:T(8,128)} %copy.25), calls=%async_computation.2 | async-start | bytes 524288 | tf_op jit(solution)/shard_map/all_to_all | solution.py:33
Sparse Core Ops, SparseCore 0:
  107.8 159.4 all-reduce.7
  270.6 58.5 all-reduce.9
  331.6 35.1 all-reduce.11
where the time goes:
time: 407 us; the launch traced here: 406 us
  waiting for transfers between devices  256 us (63%)
  blocking collectives  59 us (14%)
  other arithmetic  27.6 us (7%)
  local copies, waits for them, and re-layouts  23 us (6%)
  matrix products  21.5 us (5%)
  between operations  15.2 us (4%)
  starting transfers between devices  4.21 us (1%)
    unnamed x6, waiting for transfers between devices  250 us
    all_to_all x1, blocking collectives, on_device(): lax.all_to_all(spectra, FREQ, split_axis=0, concat_axis=2, tiled=True)  54.9 us
    dot_general x1, matrix products, on_device(): jnp.einsum('fisk,fkr->sfir', regrouped, green, preferred_element_type=jnp...  18 us
    convert_element_type x1, other arithmetic, on_device(): return result.astype(jnp.bfloat16)  12.1 us
    another operation x1, local copies, waits for them, and re-layouts, on_device(): own_share = sum_by_axis(jnp.stack([real_part, imag_part], 2), POS)  10.5 us
    sub x1, other arithmetic, on_device(): real_part = product[:, :, 0, :half_cols] - product[:, :, 1, half_cols:]  9.15 us
    unnamed x16, local copies, waits for them, and re-layouts  8.49 us
  transfers between devices with their start and end apart: 4, of which 4 were waited for; matrix products, arithmetic and copies ran while one was open for 1% of the time, Pallas kernels for 0%

commit v1 on v0

v1 whole, which is shorter than its diff:
```python
import functools

import jax
import jax.numpy as jnp
import numpy as np
from jax import lax
from jax.experimental import pallas as pl
from jax.experimental.pallas import tpu as pltpu
from jax.sharding import Mesh
from jax.sharding import PartitionSpec as P

BAND_START = 32
FREQ = ("freq_0", "freq_1")
POS = ("pos_0", "pos_1", "pos_2")
GRID = ("pos_0", "pos_1")
HOME = ("pos_0", "pos_2", "freq_0", "freq_1")
POWER = 9
GAIN = 32.0


def phase_table(total_freqs, samples):
    bins = BAND_START + np.arange(total_freqs)
    phase = bins[:, None] * np.arange(samples)[None, :] % samples
    angle = 2.0 * np.pi / samples * phase
    table = np.stack([np.cos(angle), -np.sin(angle)], 1) / np.sqrt(total_freqs)
    return table.astype(np.float32)


def swapped(block, axis):
    return lax.ppermute(block, axis, [(0, 1), (1, 0)])


def halved(value):
    high = value.astype(jnp.bfloat16)
    return high, (value - high.astype(jnp.float32)).astype(jnp.bfloat16)


def coded(value):
    scaled = value * GAIN
    square = scaled * scaled
    fourth = square * square
    return (fourth * fourth * scaled).astype(jnp.bfloat16)


def decoded(code):
    code = code.astype(jnp.float32)
    size = jnp.exp2(jnp.log2(jnp.abs(code)) * (1 / POWER)) * (1 / GAIN)
    return jnp.where(code < 0, -size, size)


def product_kernel(count, place, *refs):
    blocks, cols, out = refs[:count], refs[count], refs[-1]
    parts, shots, depth = blocks[0].shape[2:]
    half = cols.shape[2] // 2
    _, lines, _, halves, tiles, rows, width = out.shape
    spectra = jnp.concatenate([b[0, 0].reshape(parts * shots, depth) for b in blocks], 0)
    for tile in range(0, tiles, 2):
        span = slice(tile * width, (tile + 2) * width)
        shifted = slice(half + tile * width, half + (tile + 2) * width)
        with_real = jnp.dot(spectra, cols[0, :, span], preferred_element_type=jnp.float32)
        with_imag = jnp.dot(spectra, cols[0, :, shifted], preferred_element_type=jnp.float32)
        for n in range(count):
            top, low = parts * shots * n, parts * shots * n + shots
            real = with_real[top:low] - with_imag[low : low + shots]
            imag = with_imag[top:low] + with_real[low : low + shots]
            for side in range(2):
                here = slice(side * width, (side + 1) * width)
                pair = [v[:, here].reshape(lines, halves, rows // 2, width) for v in (real, imag)]
                out[0, :, n, :, tile + side] = coded(jnp.concatenate(pair, 2))


def products(place, blocks, green, span, lines, halves, groups, into=None):
    _, _, parts, shots, depth = blocks[0][0].shape
    freqs, _, columns = green.shape
    columns //= 2
    width = columns // groups
    rows = parts * shots // lines // halves
    count = len(blocks)
    begin, end = span
    spec = pl.BlockSpec

    def block_spec(array, start):
        if array.shape[0] > 1:
            return spec((1, 1, parts, shots, depth), lambda c, p: (2 * p[0] + p[1], begin - start + c, 0, 0, 0))
        return spec((1, 1, parts, shots, depth), lambda c, p: (0, begin - start + c, 0, 0, 0))

    shape = (freqs, lines, count, halves, groups, rows, width)
    extra = () if into is None else (into,)
    return pl.pallas_call(
        functools.partial(product_kernel, count),
        out_shape=jax.ShapeDtypeStruct(shape, jnp.bfloat16),
        grid_spec=pltpu.PrefetchScalarGridSpec(
            num_scalar_prefetch=1,
            grid=(end - begin,),
            in_specs=[block_spec(*b) for b in blocks]
            + [spec((1, depth, 2 * columns), lambda c, p: (begin + c, 0, 0))]
            + [spec(memory_space=pl.ANY)] * len(extra),
            out_specs=spec((1, *shape[1:]), lambda c, p: (begin + c,) + (0,) * (len(shape) - 1)),
        ),
        input_output_aliases={count + 2: 0} if extra else {},
        cost_estimate=pl.CostEstimate(
            flops=2 * (end - begin) * count * parts * shots * depth * columns * 2,
            bytes_accessed=(end - begin) * depth * columns * 4,
            transcendentals=0,
        ),
        compiler_params=pltpu.CompilerParams(vmem_limit_bytes=61 << 20),
    )(place, *[b[0] for b in blocks], green, *extra)


def passed_kernel(array, out):
    pass


def passed(array):
    anywhere = pl.BlockSpec(memory_space=pl.ANY)
    return pl.pallas_call(
        passed_kernel,
        out_shape=jax.ShapeDtypeStruct(array.shape, array.dtype),
        in_specs=[anywhere],
        out_specs=anywhere,
        input_output_aliases={0: 0},
        name="passed",
    )(array)


def filters_kernel(taps, table, out):
    shots, tap_count = taps.shape
    samples = out.shape[2]
    terms = table.shape[0]
    margin = (tap_count - 1) // 2
    shifted = [table[:, 128 + l - margin : 128 + l - margin + samples] for l in range(tap_count)]
    for s in range(shots):
        total = taps[s, 0] * shifted[0]
        for l in range(1, tap_count):
            total = total + taps[s, l] * shifted[l]
        high, low = halved(total)
        for n, value in enumerate((high, low, high)):
            out[s, n * terms : (n + 1) * terms, :] = value


def filters(filter_taps, table):
    shots = filter_taps.shape[0]
    terms, samples = table.shape
    padded = jnp.asarray(np.pad(table, ((0, 0), (128, 128))))
    return pl.pallas_call(
        filters_kernel,
        out_shape=jax.ShapeDtypeStruct((shots, 3 * terms, samples), jnp.bfloat16),
        in_specs=[
            pl.BlockSpec(memory_space=pltpu.SMEM),
            pl.BlockSpec(memory_space=pltpu.VMEM),
        ],
        out_specs=pl.BlockSpec(memory_space=pltpu.VMEM),
        cost_estimate=pl.CostEstimate(flops=2 * shots * 11 * terms * samples, bytes_accessed=2 << 20, transcendentals=0),
        name="filters",
    )(filter_taps, padded)


def subtract_kernel(sums, shaped, recorded, out, values):
    shot = pl.program_id(0)

    @pl.when(shot == 0)
    def _():
        total = sums[:, 0] + sums[:, 1]
        width = total.shape[-1]
        values[...] = jnp.swapaxes(total.reshape(-1, values.shape[0], width), 0, 1)

    high, low = halved(values[shot])
    stacked = jnp.concatenate([high, high, low], 0)
    removed = lax.dot_general(
        stacked, shaped[0], (((0,), (0,)), ((), ())), preferred_element_type=jnp.float32
    )
    out[0] = (recorded[0].astype(jnp.float32) - removed).astype(jnp.bfloat16)


def subtract(sums, shaped, recorded):
    shots, traces, samples = recorded.shape
    terms = shaped.shape[1] // 3
    spec = pl.BlockSpec
    return pl.pallas_call(
        subtract_kernel,
        out_shape=jax.ShapeDtypeStruct(recorded.shape, jnp.bfloat16),
        grid=(shots,),
        in_specs=[
            spec(sums.shape, lambda s: (0,) * sums.ndim),
            spec((1, *shaped.shape[1:]), lambda s: (s, 0, 0)),
            spec((1, traces, samples), lambda s: (s, 0, 0)),
        ],
        out_specs=spec((1, traces, samples), lambda s: (s, 0, 0)),
        scratch_shapes=[pltpu.VMEM((shots, terms, traces), jnp.float32)],
        name="subtract",
    )(sums, shaped, recorded)


def on_device(spectra, green, recorded, filter_taps):
    total_freqs, parts, shots, depth = spectra.shape
    groups = lax.axis_size(FREQ)
    own_freqs = total_freqs // groups
    lines, halves = lax.axis_size("pos_1"), lax.axis_size("pos_2")
    samples = recorded.shape[2]
    zhi, core = lax.axis_index("freq_0"), lax.axis_index("freq_1")
    place = jnp.stack([zhi, core]).astype(jnp.int32)

    table = phase_table(total_freqs, samples).reshape(groups, own_freqs, parts, samples)
    shaped = filters(filter_taps, table.swapaxes(0, 1).reshape(-1, samples))

    by_owner = spectra.reshape(groups, own_freqs, parts, shots, depth)

    def owned(array, z, c, begin=0, end=own_freqs):
        return lax.dynamic_slice_in_dim(array, (2 * z + c) * own_freqs + begin, end - begin, 0)[None]

    last = own_freqs - 1

    def sent(array, cut, axis):
        piece = cut(array)
        moved = swapped(piece, axis)
        return lax.optimization_barrier((array, piece))[0], moved

    rest, far = sent(spectra, lambda a: owned(a, 1 - zhi, core), "freq_0")
    rest, across = sent(rest, lambda a: owned(a, zhi, 1 - core), "freq_1")
    rest, cross = sent(rest, lambda a: owned(a, 1 - zhi, 1 - core, 0, last), "freq_1")
    rest, cross_last = sent(rest, lambda a: owned(a, 1 - zhi, 1 - core, last), "freq_1")
    far_across = swapped(cross, "freq_0")
    far_across_last = swapped(cross_last, "freq_0")

    def multiplied(blocks, span, into=None):
        return products(place, blocks, green, span, lines, halves, groups, into)

    def summed(part):
        part = part.reshape(-1, *part.shape[2:])
        got = lax.all_to_all(part, GRID, split_axis=0, concat_axis=0, tiled=True)
        return decoded(got).sum(0)

    part = multiplied(((by_owner, 0), (across, 0)), (0, own_freqs))
    part = passed(part)
    own = summed(part)
    part, far, shaped = lax.optimization_barrier((part, far, shaped))
    part = multiplied(((far, 0), (far_across, 0)), (0, last))
    part = multiplied(((far, 0), (far_across_last, last)), (last, own_freqs), part)
    others = summed(part)
    blocks = [own[0], own[1], others[0], others[1]]
    blocks = [jnp.where(core == 0, blocks[n], blocks[n ^ 1]) for n in range(4)]
    own = jnp.stack([jnp.where(zhi == 0, blocks[n], blocks[n ^ 2]) for n in range(4)])
    own = own.reshape(-1, *own.shape[3:])
    got = lax.all_to_all(own, HOME, split_axis=0, concat_axis=0, tiled=True)
    got = got.reshape(own_freqs, halves, groups * parts, -1, got.shape[-1])
    return subtract(got, shaped, recorded)


def solution(mesh):
    torus = Mesh(
        mesh.devices.reshape(2, 2, 4, 4, 2), ("freq_0", "freq_1", "pos_0", "pos_1", "pos_2")
    )
    placed = (P(None, None, FREQ, POS), P(FREQ, POS, None), P(POS, FREQ, None), P(POS, None))
    return jax.shard_map(on_device, mesh=torus, in_specs=placed, out_specs=P(POS, FREQ, None), check_vma=False)
```

time: 407 us -> 146 us (0.36)
  waiting for transfers between devices: 256 us -> 56.9 us
  blocking collectives: 59 us -> 16.2 us
  Pallas kernels: 0 us -> 36.4 us
  other arithmetic: 27.6 us -> 5.79 us
  matrix products: 21.5 us -> 0 us
  starting transfers between devices: 4.21 us -> 22.5 us
  local copies, waits for them, and re-layouts: 23 us -> 5.7 us
  between operations: 15.2 us -> 0.1 us
    unnamed x6 -> x0, waiting for transfers between devices: 250 us -> none
    all_to_all x2 -> x1, blocking collectives: 59 us -> 16.2 us  [on_device(): got = lax.all_to_all(own, HOME, split_axis=0, concat_axis=0, tiled=True)]
    pallas_call x0 -> x6, Pallas kernels: none -> 36.4 us  [the longest x3 25.3 us: products(): pl.pallas_call(functools.partial(product_kernel, count), out_shape=jax.Sh...]
    ppermute x0 -> x6, waiting for transfers between devices: none -> 32.4 us  [swapped(): return lax.ppermute(block, axis, [(0, 1), (1, 0)])]
    dot_general x2 -> x0, matrix products: 21.5 us -> none  [the longest x1 18 us: on_device(): jnp.einsum('fisk,fkr->sfir', regrouped, green, preferred_element_type=jnp...]
    all_to_all x1 -> x2, waiting for transfers between devices: 6.42 us -> 24.5 us  [summed(): got = lax.all_to_all(part, GRID, split_axis=0, concat_axis=0, tiled=True)]
    convert_element_type x1 -> x0, other arithmetic: 12.1 us -> none  [on_device(): return result.astype(jnp.bfloat16)]
    another operation x1 -> x0, local copies, waits for them, and re-layouts: 10.5 us -> none  [on_device(): own_share = sum_by_axis(jnp.stack([real_part, imag_part], 2), POS)]
  transfers between devices with their start and end apart: 4 -> 8, of which waited for: 4 -> 4; matrix products, arithmetic and copies ran while one was open for 1% -> 4% of each run, Pallas kernels for 0% -> 20%
where the time goes in v1:
time: 146 us; the launch traced here: 144 us
  waiting for transfers between devices  56.9 us (39%)
  Pallas kernels  36.4 us (25%)
  starting transfers between devices  22.5 us (15%)
  blocking collectives  16.2 us (11%)
  other arithmetic  5.79 us (4%)
  local copies, waits for them, and re-layouts  5.7 us (4%)
    ppermute x6, waiting for transfers between devices, swapped(): return lax.ppermute(block, axis, [(0, 1), (1, 0)])  32.4 us
    pallas_call x3, Pallas kernels, products(): pl.pallas_call(functools.partial(product_kernel, count), out_shape=jax.Sh...  25.3 us
    all_to_all x2, waiting for transfers between devices, summed(): got = lax.all_to_all(part, GRID, split_axis=0, concat_axis=0, tiled=True)  24.5 us
    all_to_all x1, blocking collectives, on_device(): got = lax.all_to_all(own, HOME, split_axis=0, concat_axis=0, tiled=True)  16.2 us
    all_to_all x2, starting transfers between devices, summed(): got = lax.all_to_all(part, GRID, split_axis=0, concat_axis=0, tiled=True)  14.3 us
    ppermute x6, starting transfers between devices, swapped(): return lax.ppermute(block, axis, [(0, 1), (1, 0)])  8.23 us
    pallas_call x1, Pallas kernels, subtract(): pl.pallas_call(subtract_kernel, out_shape=jax.ShapeDtypeStruct(recorded.s...  6.98 us
    reduce_sum x2, other arithmetic, summed(): return decoded(got).sum(0)  5.04 us
  transfers between devices with their start and end apart: 8, of which 4 were waited for; matrix products, arithmetic and copies ran while one was open for 4% of the time, Pallas kernels for 20%

profile of v1, /device:TPU:0, one launch (start us, length us, event | category | flops | bytes accessed | tf_op | source)
XLA Modules:
  0.0 143.7 jit_solution(4071068169453735606)
XLA Ops:
  0.0 1.3 dynamic-slice_bitcast_fusion.1
  1.3 1.3 dynamic-slice_bitcast_fusion
  2.6 0.1 collective-permute-start
  2.7 1.2 dynamic-slice_bitcast_fusion.2
  4.0 0.6 collective-permute-start.4
  4.5 0.7 pad_add_fusion.place
  5.2 0.3 collective-permute-done.refs_1_
  5.5 10.8 %shard_map.55.array = bf16[4,4,2,2,4,16,256]{6,5,4,3,2,1,0:T(8,128)(2,1)} custom-call(s32[2]{0:T(128)} %pad_add_fusion.place, bf16[4,4,2,64,1024]{4,3,2,1,0:T(8,128)(2,1)} %bitcast.17, bf16[1,4,2,64,1024]{4,3,2,1,0:T(8,128)(2,1)} %collective-permute-done.refs_1_, bf16[4,1024,2048]{2,1,0:T(8,128)(2,1)} %refs_2_.5), custom_call_target="tpu_custom_call" | custom-call | flops 4294967296 | bytes 16777216 | tf_op jit(solution)/shard_map/pallas_call | solution.py:89
  16.3 7.2 %all-to-all-start = ((bf16[16,2,2,4,16,256]{5,4,3,2,1,0:T(8,128)(2,1)}), bf16[16,2,2,4,16,256]{5,4,3,2,1,0:T(8,128)(2,1)}, u32[]{:S(2)}, u32[]{:S(2)}) async-start(bf16[16,2,2,4,16,256]{5,4,3,2,1,0:T(8,128)(2,1)} %bitcast.16), calls=%async_computation | async-start | bytes 4194304 | tf_op jit(solution)/shard_map/all_to_all | solution.py:230
  23.6 4.0 %collective-permute-start.1 = (bf16[1,4,2,64,1024]{4,3,2,1,0:T(8,128)(2,1)S(1)}, bf16[1,4,2,64,1024]{4,3,2,1,0:T(8,128)(2,1)S(1)}, u32[]{:S(2)}, u32[]{:S(2)}) collective-permute-start(bf16[1,4,2,64,1024]{4,3,2,1,0:T(8,128)(2,1)S(1)} %dynamic-slice_bitcast_fusion.1), channel_id=1, source_target_pairs={{0,64},{64,0},{1,65},{65,1},{2,66},{66,2},{3,67},{67,3},{4,68},{68... | collective-permute-start | bytes 3145736 | tf_op jit(solution)/shard_map/ppermute | solution.py:30
  27.5 0.0 collective-permute-done.4
  27.5 0.1 collective-permute-start.5
  27.6 1.0 dynamic-slice_bitcast_fusion.3
  28.6 0.1 collective-permute-start.2
  28.7 4.2 %filters.1.shaped = bf16[8,96,512]{2,1,0:T(8,128)(2,1)} custom-call(f32[8,11]{1,0:T(8,128)} %taps.1, f32[32,768]{1,0:T(8,128)} %constant.39.clone.table), custom_call_target="tpu_custom_call" | custom-call | flops 2883584 | bytes 2097152 | tf_op jit(solution)/shard_map/filters/pallas_call | solution.py:145
  32.9 0.0 collective-permute-done.2
  32.9 3.4 %collective-permute-start.3 = (bf16[1,1,2,64,1024]{4,3,2,1,0:T(8,128)(2,1)}, bf16[1,1,2,64,1024]{4,3,2,1,0:T(8,128)(2,1)}, u32[]{:S(2)}, u32[]{:S(2)}) collective-permute-start(bf16[1,1,2,64,1024]{4,3,2,1,0:T(8,128)(2,1)} %collective-permute-done.2), channel_id=1, source_target_pairs={{0,64},{64,0},{1,65},{65,1},{2,66},{66,2},{3,67},{67,3},{4,68},{68... | collective-permute-start | bytes 786440 | tf_op jit(solution)/shard_map/ppermute | solution.py:30
  36.3 15.2 %collective-permute-done.1.refs_0_ = bf16[1,4,2,64,1024]{4,3,2,1,0:T(8,128)(2,1)S(1)} collective-permute-done((bf16[1,4,2,64,1024]{4,3,2,1,0:T(8,128)(2,1)S(1)}, bf16[1,4,2,64,1024]{4,3,2,1,0:T(8,128)(2,1)S(1)}, u32[]{:S(2)}, u32[]{:S(2)}) %collective-permute-start.1) | collective-permute-done | bytes 1048608 | tf_op jit(solution)/shard_map/ppermute | solution.py:30
  51.5 16.9 %collective-permute-done.5.refs_1_ = bf16[1,3,2,64,1024]{4,3,2,1,0:T(8,128)(2,1)S(1)} collective-permute-done((bf16[1,3,2,64,1024]{4,3,2,1,0:T(8,128)(2,1)}, bf16[1,3,2,64,1024]{4,3,2,1,0:T(8,128)(2,1)S(1)}, u32[]{:S(2)}, u32[]{:S(2)}) %collective-permute-start.5) | collective-permute-done | bytes 786464 | tf_op jit(solution)/shard_map/ppermute | solution.py:30
  68.4 0.0 copy-done
  68.4 0.9 copy-done.1
  69.3 9.3 %shard_map.56.refs_3_ = bf16[4,4,2,2,4,16,256]{6,5,4,3,2,1,0:T(8,128)(2,1)} custom-call(s32[2]{0:T(128)} %pad_add_fusion.place, bf16[1,4,2,64,1024]{4,3,2,1,0:T(8,128)(2,1)} %copy-done, bf16[1,3,2,64,1024]{4,3,2,1,0:T(8,128)(2,1)} %copy-done.1, bf16[4,1024,2048]{2,1,0:T(8,128)(2,1)} %refs_2_.5), custom_call_target="tpu_custom_call" | custom-call | flops 3221225472 | bytes 12582912 | tf_op jit(solution)/shard_map/pallas_call | solution.py:89
  78.6 0.0 collective-permute-done.3.refs_1_
  78.6 5.2 %shard_map.57 = bf16[4,4,2,2,4,16,256]{6,5,4,3,2,1,0:T(8,128)(2,1)} custom-call(s32[2]{0:T(128)} %pad_add_fusion.place, bf16[1,4,2,64,1024]{4,3,2,1,0:T(8,128)(2,1)} %copy-done, bf16[1,1,2,64,1024]{4,3,2,1,0:T(8,128)(2,1)} %collective-permute-done.3.refs_1_, bf16[4,1024,2048]{2,1,0:T(8,128)(2,1)} %refs_2_.5, ...), custom_call_target="tpu_custom_call", output_to_operand_aliasing={{}: (4, {})} | custom-call | flops 1073741824 | bytes 4194304 | tf_op jit(solution)/shard_map/pallas_call | solution.py:89
  83.7 0.0 all-to-all-done
  83.7 7.1 %all-to-all-start.1 = ((bf16[16,2,2,4,16,256]{5,4,3,2,1,0:T(8,128)(2,1)}), bf16[16,2,2,4,16,256]{5,4,3,2,1,0:T(8,128)(2,1)S(1)}, u32[]{:S(2)}, u32[]{:S(2)}) async-start(bf16[16,2,2,4,16,256]{5,4,3,2,1,0:T(8,128)(2,1)} %bitcast.15), calls=%async_computation.1 | async-start | bytes 4194304 | tf_op jit(solution)/shard_map/all_to_all | solution.py:230
  90.8 3.3 %fusion.8 = f32[2,2,4,16,256]{4,3,2,1,0:T(8,128)S(1)} fusion(bf16[16,2,2,4,16,256]{5,4,3,2,1,0:T(8,128)(2,1)} %all-to-all-done), kind=kLoop, calls=%fused_computation.14 | loop fusion | flops 8323072 | bytes 2359296 | tf_op jit(solution)/shard_map/reduce_sum | solution.py:231
  94.2 24.5 %all-to-all-done.1 = bf16[16,2,2,4,16,256]{5,4,3,2,1,0:T(8,128)(2,1)S(1)} async-done(((bf16[16,2,2,4,16,256]{5,4,3,2,1,0:T(8,128)(2,1)}), bf16[16,2,2,4,16,256]{5,4,3,2,1,0:T(8,128)(2,1)S(1)}, u32[]{:S(2)}, u32[]{:S(2)}) %all-to-all-start.1) | async-done | bytes 2097184 | tf_op jit(solution)/shard_map/all_to_all | solution.py:230
  118.7 1.7 %fusion.9 = f32[2,2,4,16,256]{4,3,2,1,0:T(8,128)S(1)} fusion(bf16[16,2,2,4,16,256]{5,4,3,2,1,0:T(8,128)(2,1)S(1)} %all-to-all-done.1), kind=kLoop, calls=%fused_computation.15 | loop fusion | flops 8323072 | bytes 2359296 | tf_op jit(solution)/shard_map/reduce_sum | solution.py:231
  120.4 0.1 broadcast_select_fusion.3
  120.5 16.2 %all_to_all.15 = f32[32,16,256]{2,1,0:T(8,128)} all-to-all(f32[32,16,256]{2,1,0:T(8,128)S(1)} %bitcast.18), channel_id=1, replica_groups=mesh['freq_0'=2,'freq_1'=2,'pos_0'=4,'pos_1'=4,'pos_2'=2] {'pos_0','pos_..., dimensions={0} | all-to-all | bytes 1048576 | tf_op jit(solution)/shard_map/all_to_all | solution.py:244
  136.7 7.0 %subtract.1 = bf16[8,256,512]{2,1,0:T(8,128)(2,1)} custom-call(f32[4,2,8,8,256]{4,3,2,1,0:T(8,128)} %bitcast.19, bf16[8,96,512]{2,1,0:T(8,128)(2,1)} %filters.1.shaped, bf16[8,256,512]{2,1,0:T(8,128)(2,1)} %recorded.1), custom_call_target="tpu_custom_call" | custom-call | tf_op jit(solution)/shard_map/subtract/pallas_call | solution.py:179
  (4 shorter events, 0.0 us)
Async XLA Ops:
  2.6 2.9 %collective-permute-start = (bf16[1,4,2,64,1024]{4,3,2,1,0:T(8,128)(2,1)S(1)}, bf16[1,4,2,64,1024]{4,3,2,1,0:T(8,128)(2,1)}, u32[]{:S(2)}, u32[]{:S(2)}) collective-permute-start(bf16[1,4,2,64,1024]{4,3,2,1,0:T(8,128)(2,1)S(1)} %dynamic-slice_bitcast_fusion), channel_id=1, source_target_pairs={{0,32},{32,0},{1,33},{33,1},{2,34},{34,2},{3,35},{35,3},{4,36},{36... | collective-permute-start | bytes 3145736 | tf_op jit(solution)/shard_map/ppermute | solution.py:30
  4.0 23.6 %collective-permute-start.4 = (bf16[1,3,2,64,1024]{4,3,2,1,0:T(8,128)(2,1)S(1)}, bf16[1,3,2,64,1024]{4,3,2,1,0:T(8,128)(2,1)}, u32[]{:S(2)}, u32[]{:S(2)}) collective-permute-start(bf16[1,3,2,64,1024]{4,3,2,1,0:T(8,128)(2,1)S(1)} %dynamic-slice_bitcast_fusion.2), channel_id=1, source_target_pairs={{0,32},{32,0},{1,33},{33,1},{2,34},{34,2},{3,35},{35,3},{4,36},{36... | collective-permute-start | bytes 2359304 | tf_op jit(solution)/shard_map/ppermute | solution.py:30
  16.3 67.4 %all-to-all-start = ((bf16[16,2,2,4,16,256]{5,4,3,2,1,0:T(8,128)(2,1)}), bf16[16,2,2,4,16,256]{5,4,3,2,1,0:T(8,128)(2,1)}, u32[]{:S(2)}, u32[]{:S(2)}) async-start(bf16[16,2,2,4,16,256]{5,4,3,2,1,0:T(8,128)(2,1)} %bitcast.16), calls=%async_computation | async-start | bytes 4194304 | tf_op jit(solution)/shard_map/all_to_all | solution.py:230
  23.6 28.0 %collective-permute-start.1 = (bf16[1,4,2,64,1024]{4,3,2,1,0:T(8,128)(2,1)S(1)}, bf16[1,4,2,64,1024]{4,3,2,1,0:T(8,128)(2,1)S(1)}, u32[]{:S(2)}, u32[]{:S(2)}) collective-permute-start(bf16[1,4,2,64,1024]{4,3,2,1,0:T(8,128)(2,1)S(1)} %dynamic-slice_bitcast_fusion.1), channel_id=1, source_target_pairs={{0,64},{64,0},{1,65},{65,1},{2,66},{66,2},{3,67},{67,3},{4,68},{68... | collective-permute-start | bytes 3145736 | tf_op jit(solution)/shard_map/ppermute | solution.py:30
  27.5 40.9 %collective-permute-start.5 = (bf16[1,3,2,64,1024]{4,3,2,1,0:T(8,128)(2,1)}, bf16[1,3,2,64,1024]{4,3,2,1,0:T(8,128)(2,1)S(1)}, u32[]{:S(2)}, u32[]{:S(2)}) collective-permute-start(bf16[1,3,2,64,1024]{4,3,2,1,0:T(8,128)(2,1)} %collective-permute-done.4), channel_id=1, source_target_pairs={{0,64},{64,0},{1,65},{65,1},{2,66},{66,2},{3,67},{67,3},{4,68},{68... | collective-permute-start | bytes 2359304 | tf_op jit(solution)/shard_map/ppermute | solution.py:30
  28.6 4.3 %collective-permute-start.2 = (bf16[1,1,2,64,1024]{4,3,2,1,0:T(8,128)(2,1)S(1)}, bf16[1,1,2,64,1024]{4,3,2,1,0:T(8,128)(2,1)}, u32[]{:S(2)}, u32[]{:S(2)}) collective-permute-start(bf16[1,1,2,64,1024]{4,3,2,1,0:T(8,128)(2,1)S(1)} %dynamic-slice_bitcast_fusion.3), channel_id=1, source_target_pairs={{0,32},{32,0},{1,33},{33,1},{2,34},{34,2},{3,35},{35,3},{4,36},{36... | collective-permute-start | bytes 786440 | tf_op jit(solution)/shard_map/ppermute | solution.py:30
  32.9 45.7 %collective-permute-start.3 = (bf16[1,1,2,64,1024]{4,3,2,1,0:T(8,128)(2,1)}, bf16[1,1,2,64,1024]{4,3,2,1,0:T(8,128)(2,1)}, u32[]{:S(2)}, u32[]{:S(2)}) collective-permute-start(bf16[1,1,2,64,1024]{4,3,2,1,0:T(8,128)(2,1)} %collective-permute-done.2), channel_id=1, source_target_pairs={{0,64},{64,0},{1,65},{65,1},{2,66},{66,2},{3,67},{67,3},{4,68},{68... | collective-permute-start | bytes 786440 | tf_op jit(solution)/shard_map/ppermute | solution.py:30
  51.5 16.9 %copy-start = (bf16[1,4,2,64,1024]{4,3,2,1,0:T(8,128)(2,1)}, bf16[1,4,2,64,1024]{4,3,2,1,0:T(8,128)(2,1)S(1)}, u32[]{:S(2)}) copy-start(bf16[1,4,2,64,1024]{4,3,2,1,0:T(8,128)(2,1)S(1)} %collective-permute-done.1.refs_0_) | copy-start | bytes 3145732
  68.4 0.9 copy-start.1
  83.7 35.0 %all-to-all-start.1 = ((bf16[16,2,2,4,16,256]{5,4,3,2,1,0:T(8,128)(2,1)}), bf16[16,2,2,4,16,256]{5,4,3,2,1,0:T(8,128)(2,1)S(1)}, u32[]{:S(2)}, u32[]{:S(2)}) async-start(bf16[16,2,2,4,16,256]{5,4,3,2,1,0:T(8,128)(2,1)} %bitcast.15), calls=%async_computation.1 | async-start | bytes 4194304 | tf_op jit(solution)/shard_map/all_to_all | solution.py:230

commit v2 on v1

v2 whole, which is shorter than its diff:
```python
import functools

import jax
import jax.numpy as jnp
import numpy as np
from jax import lax
from jax.experimental import pallas as pl
from jax.experimental.pallas import tpu as pltpu
from jax.sharding import Mesh
from jax.sharding import PartitionSpec as P

BAND_START = 32
FREQ = ("freq_0", "freq_1")
POS = ("pos_0", "pos_1", "pos_2")
GRID = ("pos_0", "pos_1")
HOME = ("pos_0", "pos_2", "freq_0", "freq_1")
GAIN = 64.0


def phase_table(total_freqs, samples):
    bins = BAND_START + np.arange(total_freqs)
    phase = bins[:, None] * np.arange(samples)[None, :] % samples
    angle = 2.0 * np.pi / samples * phase
    table = np.stack([np.cos(angle), -np.sin(angle)], 1) / np.sqrt(total_freqs)
    return table.astype(np.float32)


def swapped(block, axis):
    return lax.ppermute(block, axis, [(0, 1), (1, 0)])


def halved(value):
    high = value.astype(jnp.bfloat16)
    return high, (value - high.astype(jnp.float32)).astype(jnp.bfloat16)


def coded(value):
    scaled = value * GAIN
    square = scaled * scaled
    fourth = square * square
    return (fourth * scaled * jnp.maximum(fourth, 256.0)).astype(jnp.bfloat16)


def decoded(code):
    code = code.astype(jnp.float32)
    power = jnp.log2(jnp.abs(code))
    size = jnp.exp2(jnp.minimum(power * (1 / 9), (power - 8.0) * (1 / 5))) * (1 / GAIN)
    return jnp.where(code < 0, -size, size)


def sums_kernel(far, code, *refs):
    out, code_in, totals, in_sems, out_sems = refs[-5:]
    zhi, core = lax.axis_index("freq_0"), lax.axis_index("freq_1")
    first = 2 * (1 - zhi if far else zhi)
    places = (first + core, first + 1 - core)
    _, slots, halves, groups = code.shape[:4]
    pieces = [(slot, half) for slot in range(slots) for half in range(halves)]

    def load(n):
        slot, half = pieces[n]
        return pltpu.make_async_copy(code.at[:, slot, half], code_in.at[n], in_sems.at[n])

    def store(n):
        slot, half = pieces[n]
        return pltpu.make_async_copy(totals.at[n], out.at[places[slot], half], out_sems.at[n])

    for n in range(len(pieces)):
        load(n).start()
    for n in range(len(pieces)):
        load(n).wait()

        def step(g, carry):
            total = decoded(code_in[n, 0, g])
            for source in range(1, code_in.shape[1]):
                total = total + decoded(code_in[n, source, g])
            totals[n, g] = total
            return carry

        lax.fori_loop(0, groups, step, 0)
        store(n).start()
    for n in range(len(pieces)):
        store(n).wait()


def sums(code, far, into=None):
    sources, slots, halves, *rest = code.shape
    extra = () if into is None else (into,)
    anywhere = pl.BlockSpec(memory_space=pl.ANY)
    pieces = slots * halves
    return pl.pallas_call(
        functools.partial(sums_kernel, far),
        out_shape=jax.ShapeDtypeStruct((2 * slots, halves, *rest), jnp.float32),
        in_specs=[anywhere] * (1 + len(extra)),
        out_specs=anywhere,
        input_output_aliases={1: 0} if extra else {},
        scratch_shapes=[
            pltpu.VMEM((pieces, sources, *rest), code.dtype),
            pltpu.VMEM((pieces, *rest), jnp.float32),
            pltpu.SemaphoreType.DMA((pieces,)),
            pltpu.SemaphoreType.DMA((pieces,)),
        ],
        cost_estimate=pl.CostEstimate(flops=12 << 20, bytes_accessed=3 << 20, transcendentals=2 << 20),
        compiler_params=pltpu.CompilerParams(vmem_limit_bytes=(61 if far else 40) << 20),
        name="sums",
    )(code, *extra)


def cut_kernel(spectra, far, across, *rest):
    *pieces, sems = rest
    zhi, core = lax.axis_index("freq_0"), lax.axis_index("freq_1")
    freqs = across.shape[0]
    start = (2 * (1 - zhi) + core) * freqs
    copies = [pltpu.make_async_copy(spectra.at[pl.ds(start, freqs)], far, sems.at[len(pieces) + 1])]
    start = (2 * zhi + 1 - core) * freqs
    copies.append(pltpu.make_async_copy(spectra.at[pl.ds(start, freqs)], across, sems.at[0]))
    start = (2 * (1 - zhi) + 1 - core) * freqs
    for n, piece in enumerate(pieces):
        copies.append(pltpu.make_async_copy(spectra.at[pl.ds(start, piece.shape[0])], piece, sems.at[n + 1]))
        start = start + piece.shape[0]
    for copy in copies:
        copy.start()
    for copy in copies:
        copy.wait()


def cut(spectra, own_freqs, counts):
    counts = (own_freqs, own_freqs, *counts)
    return pl.pallas_call(
        cut_kernel,
        out_shape=[jax.ShapeDtypeStruct((n, *spectra.shape[1:]), spectra.dtype) for n in counts],
        in_specs=[pl.BlockSpec(memory_space=pltpu.HBM)],
        out_specs=[pl.BlockSpec(memory_space=pltpu.VMEM)] * len(counts),
        scratch_shapes=[pltpu.SemaphoreType.DMA((len(counts),))],
        compiler_params=pltpu.CompilerParams(vmem_limit_bytes=61 << 20),
        name="cut",
    )(spectra)


def multiply(blocks, cols, write, lines, halves, groups):
    parts, shots, depth = blocks[0].shape
    half = cols.shape[1] // 2
    width = half // groups
    rows = jnp.concatenate([b.reshape(parts * shots, depth) for b in blocks], 0)
    for tile in range(0, groups, 2):
        span = slice(tile * width, (tile + 2) * width)
        shifted = slice(half + tile * width, half + (tile + 2) * width)
        with_real = jnp.dot(rows, cols[:, span], preferred_element_type=jnp.float32)
        with_imag = jnp.dot(rows, cols[:, shifted], preferred_element_type=jnp.float32)
        for slot in range(len(blocks)):
            top = slot * parts * shots
            middle, end = top + shots, top + parts * shots
            real = with_real[top:middle] - with_imag[middle:end]
            imag = with_imag[top:middle] + with_real[middle:end]
            for side in range(2):
                here = slice(side * width, (side + 1) * width)
                pair = [v[:, here].reshape(lines, halves, -1, width) for v in (real, imag)]
                write(slot, tile + side, coded(jnp.concatenate(pair, 2)))


def block_kernel(begin, first_slot, slots, green, *refs):
    blocks = refs[:slots]
    out, blocks_in, green_in, codes, block_sems, green_sems, code_sems = refs[-7:]
    count = green_in.shape[0]
    owner = 2 * lax.axis_index("freq_0") + lax.axis_index("freq_1")

    def loads(n):
        copies = [pltpu.make_async_copy(green.at[begin + n], green_in.at[n], green_sems.at[n])]
        for slot, block in enumerate(blocks):
            at = owner * green.shape[0] + n if block.shape[0] > green.shape[0] else n
            copies.append(pltpu.make_async_copy(block.at[at], blocks_in.at[slot, n], block_sems.at[slot, n]))
        return copies

    def store(n):
        return pltpu.make_async_copy(codes.at[n], out.at[begin + n, :, pl.ds(first_slot, slots)], code_sems.at[n])

    for n in range(count):
        for copy in loads(n):
            copy.start()

    def step(n, carry):
        for copy in loads(n):
            copy.wait()

        def write(slot, tile, code):
            codes[n, :, slot, :, tile] = code

        _, lines, _, halves, groups = codes.shape[:5]
        multiply([blocks_in[slot, n] for slot in range(slots)], green_in.at[n], write, lines, halves, groups)
        store(n).start()
        return carry

    lax.fori_loop(0, count, step, 0)
    for n in range(count):
        store(n).wait()


def block_products(blocks, green, begin, count, slot, shape, into=None):
    parts, shots, depth = blocks[0].shape[1:]
    slots = len(blocks)
    extra = () if into is None else (into,)
    hbm, anywhere = (pl.BlockSpec(memory_space=m) for m in (pltpu.HBM, pl.ANY))
    flops = 4 * slots * count * parts * shots * depth * green.shape[2] // 2
    return pl.pallas_call(
        functools.partial(block_kernel, begin, slot, slots),
        out_shape=jax.ShapeDtypeStruct(shape, jnp.bfloat16),
        in_specs=[hbm] + [anywhere] * slots + [hbm] * len(extra),
        out_specs=hbm,
        input_output_aliases={} if into is None else {1 + slots: 0},
        scratch_shapes=[
            pltpu.VMEM((slots, count, parts, shots, depth), blocks[0].dtype),
            pltpu.VMEM((count, *green.shape[1:]), green.dtype),
            pltpu.VMEM((count, shape[1], slots, *shape[3:]), jnp.bfloat16),
            pltpu.SemaphoreType.DMA((slots, count)),
            pltpu.SemaphoreType.DMA((count,)),
            pltpu.SemaphoreType.DMA((count,)),
        ],
        cost_estimate=pl.CostEstimate(flops=flops, bytes_accessed=count << 22, transcendentals=0),
        compiler_params=pltpu.CompilerParams(vmem_limit_bytes=61 << 20),
    )(green, *blocks, *extra)


def filters_kernel(taps, table, out):
    shots, tap_count = taps.shape
    samples = out.shape[2]
    terms = table.shape[0]
    margin = (tap_count - 1) // 2
    shifted = [table[:, 128 + l - margin : 128 + l - margin + samples] for l in range(tap_count)]
    for s in range(shots):
        total = taps[s, 0] * shifted[0]
        for l in range(1, tap_count):
            total = total + taps[s, l] * shifted[l]
        high, low = halved(total)
        for n, value in enumerate((high, low, high)):
            out[s, n * terms : (n + 1) * terms, :] = value


def filters(filter_taps, table):
    shots = filter_taps.shape[0]
    terms, samples = table.shape
    padded = jnp.asarray(np.pad(table, ((0, 0), (128, 128))))
    return pl.pallas_call(
        filters_kernel,
        out_shape=jax.ShapeDtypeStruct((shots, 3 * terms, samples), jnp.bfloat16),
        in_specs=[
            pl.BlockSpec(memory_space=pltpu.SMEM),
            pl.BlockSpec(memory_space=pltpu.VMEM),
        ],
        out_specs=pl.BlockSpec(memory_space=pltpu.VMEM),
        cost_estimate=pl.CostEstimate(flops=2 * shots * 11 * terms * samples, bytes_accessed=2 << 20, transcendentals=0),
        compiler_params=pltpu.CompilerParams(vmem_limit_bytes=8 << 20),
        name="filters",
    )(filter_taps, padded)


def subtract_kernel(sums, shaped, recorded, out, values):
    @pl.when(pl.program_id(0) == 0)
    def _():
        total = sums[:, 0] + sums[:, 1]
        width = total.shape[-1]
        values[...] = jnp.swapaxes(total.reshape(-1, values.shape[0], width), 0, 1)

    for n in range(out.shape[0]):
        high, low = halved(values[pl.program_id(0) * out.shape[0] + n])
        stacked = jnp.concatenate([high, high, low], 0)
        removed = lax.dot_general(
            stacked, shaped[n], (((0,), (0,)), ((), ())), preferred_element_type=jnp.float32
        )
        out[n] = (recorded[n].astype(jnp.float32) - removed).astype(jnp.bfloat16)


def subtract(sums, shaped, recorded):
    shots, traces, samples = recorded.shape
    terms = shaped.shape[1] // 3
    spec = pl.BlockSpec
    step = 2
    return pl.pallas_call(
        subtract_kernel,
        out_shape=jax.ShapeDtypeStruct(recorded.shape, jnp.bfloat16),
        grid=(shots // step,),
        in_specs=[
            spec(memory_space=pltpu.VMEM),
            spec((step, *shaped.shape[1:]), lambda s: (s, 0, 0)),
            spec((step, traces, samples), lambda s: (s, 0, 0)),
        ],
        out_specs=spec((step, traces, samples), lambda s: (s, 0, 0)),
        scratch_shapes=[pltpu.VMEM((shots, terms, traces), jnp.float32)],
        compiler_params=pltpu.CompilerParams(vmem_limit_bytes=16 << 20),
        name="subtract",
    )(sums, shaped, recorded)


def on_device(spectra, green, recorded, filter_taps):
    total_freqs, parts, shots, _ = spectra.shape
    groups = lax.axis_size(FREQ)
    own_freqs = total_freqs // groups
    lines, halves = lax.axis_size("pos_1"), lax.axis_size("pos_2")
    samples = recorded.shape[2]
    table = phase_table(total_freqs, samples).reshape(groups, own_freqs, parts, samples)
    shaped = filters(filter_taps, table.swapaxes(0, 1).reshape(-1, samples))

    counts = (own_freqs - 2, 1, 1)

    far, across, *pieces = cut(spectra, own_freqs, counts)
    far = swapped(far, "freq_0")
    across = swapped(across, "freq_1")
    pieces = [swapped(piece, "freq_1") for piece in pieces]
    pieces = [swapped(piece, "freq_0") for piece in pieces]

    def scattered(part):
        part = part.reshape(-1, *part.shape[2:])
        return lax.all_to_all(part, GRID, split_axis=0, concat_axis=0, tiled=True)

    shape = (own_freqs, lines, 2, halves, groups, parts * shots // lines // halves, green.shape[2] // 2 // groups)
    part = block_products((spectra, across), green, 0, own_freqs, 0, shape)
    total = sums(scattered(part), False)
    part, far, shaped = lax.optimization_barrier((part, far, shaped))
    part = block_products((far,), green, 0, own_freqs, 0, shape)
    begin = 0
    for piece, count in zip(pieces, counts):
        part = block_products((piece,), green, begin, count, 1, shape, part)
        begin += count
    total = sums(scattered(part), True, total)
    total = total.reshape(-1, *total.shape[3:])
    got = lax.all_to_all(total, HOME, split_axis=0, concat_axis=0, tiled=True)
    got = got.reshape(own_freqs, halves, groups * parts, -1, got.shape[-1])
    return subtract(got, shaped, recorded)


def solution(mesh):
    torus = Mesh(
        mesh.devices.reshape(2, 2, 4, 4, 2), ("freq_0", "freq_1", "pos_0", "pos_1", "pos_2")
    )
    placed = (P(None, None, FREQ, POS), P(FREQ, POS, None), P(POS, FREQ, None), P(POS, None))
    return jax.shard_map(on_device, mesh=torus, in_specs=placed, out_specs=P(POS, FREQ, None), check_vma=False)
```

time: 146 us -> 142 us (0.973)
  Pallas kernels: 36.4 us -> 44.8 us
  other arithmetic: 5.79 us -> 0 us
  local copies, waits for them, and re-layouts: 5.7 us -> 1.79 us
  waiting for transfers between devices: 56.9 us -> 54.3 us
    pallas_call x4 -> x8, Pallas kernels: 25.3 us -> 39.2 us  [the longest x5 29.5 us: block_products(): pl.pallas_call(functools.partial(block_kernel, begin, slot, slots), out_s...]
    reduce_sum x2 -> x0, other arithmetic: 5.04 us -> none  [summed(): return decoded(got).sum(0)]
    broadcast_in_dim x4 -> x0, local copies, waits for them, and re-layouts: 4.8 us -> none  [owned(): lax.dynamic_slice_in_dim(array, (2 * z + c) * own_freqs + begin, end - be...]
    pallas_call x1, Pallas kernels: 6.98 us -> 2.63 us  [subtract(): pl.pallas_call(subtract_kernel, out_shape=jax.ShapeDtypeStruct(recorded.s...]
    ppermute x6 -> x8, waiting for transfers between devices: 32.4 us -> 28.6 us  [swapped(): return lax.ppermute(block, axis, [(0, 1), (1, 0)])]
    ppermute x6 -> x8, starting transfers between devices: 8.23 us -> 8.27 us  [swapped(): return lax.ppermute(block, axis, [(0, 1), (1, 0)])]
  transfers between devices with their start and end apart: 8 -> 10, of which waited for: 4 -> 6; matrix products, arithmetic and copies ran while one was open for 4% -> 0% of each run, Pallas kernels for 20% -> 18%
where the time goes in v2:
time: 142 us; the launch traced here: 140 us
  waiting for transfers between devices  54.3 us (38%)
  Pallas kernels  44.8 us (32%)
  starting transfers between devices  22.5 us (16%)
  blocking collectives  16.6 us (12%)
  local copies, waits for them, and re-layouts  1.79 us (1%)
    pallas_call x5, Pallas kernels, block_products(): pl.pallas_call(functools.partial(block_kernel, begin, slot, slots), out_s...  29.5 us
    ppermute x8, waiting for transfers between devices, swapped(): return lax.ppermute(block, axis, [(0, 1), (1, 0)])  28.6 us
    all_to_all x2, waiting for transfers between devices, scattered(): return lax.all_to_all(part, GRID, split_axis=0, concat_axis=0, tiled=True)  25.7 us
    all_to_all x1, blocking collectives, on_device(): got = lax.all_to_all(total, HOME, split_axis=0, concat_axis=0, tiled=True)  16.6 us
    all_to_all x2, starting transfers between devices, scattered(): return lax.all_to_all(part, GRID, split_axis=0, concat_axis=0, tiled=True)  14.2 us
    ppermute x8, starting transfers between devices, swapped(): return lax.ppermute(block, axis, [(0, 1), (1, 0)])  8.27 us
    pallas_call x2, Pallas kernels, sums(): pl.pallas_call(functools.partial(sums_kernel, far), out_shape=jax.ShapeDt...  6.18 us
    pallas_call x1, Pallas kernels, cut(): pl.pallas_call(cut_kernel, out_shape=[jax.ShapeDtypeStruct((n, *spectra.s...  3.5 us
  transfers between devices with their start and end apart: 10, of which 6 were waited for; matrix products, arithmetic and copies ran while one was open for 0% of the time, Pallas kernels for 18%

profile of v2, /device:TPU:0, one launch (start us, length us, event | category | flops | bytes accessed | tf_op | source)
XLA Modules:
  0.0 140.1 jit_solution(16937249618951785325)
XLA Ops:
  0.0 3.5 %cut.1 = (bf16[4,2,64,1024]{3,2,1,0:T(8,128)(2,1)}, bf16[4,2,64,1024]{3,2,1,0:T(8,128)(2,1)}, bf16[2,2,64,1024]{3,2,1,0:T(8,128)(2,1)}, bf16[1,2,64,1024]{3,2,1,0:T(8,128)(2,1)}, bf16[1,2,64,1024]{3,2,1,0:T(8,128)(2,1)}) custom-call(bf16[16,2,64,1024]{3,2,1,0:T(8,128)(2,1)} %refs_0_.1), custom_call_target="tpu_custom_call" | custom-call | tf_op jit(solution)/shard_map/cut/pallas_call | solution.py:128
  3.5 0.1 collective-permute-start.6
  3.6 2.9 %collective-permute-done.6.refs_1_ = bf16[4,2,64,1024]{3,2,1,0:T(8,128)(2,1)S(1)} collective-permute-done((bf16[4,2,64,1024]{3,2,1,0:T(8,128)(2,1)}, bf16[4,2,64,1024]{3,2,1,0:T(8,128)(2,1)S(1)}, u32[]{:S(2)}, u32[]{:S(2)}) %collective-permute-start.6) | collective-permute-done | bytes 1048608 | tf_op jit(solution)/shard_map/ppermute | solution.py:29
  6.5 1.0 copy-done.4
  7.4 9.1 %shard_map.55 = bf16[4,4,2,2,4,16,256]{6,5,4,3,2,1,0:T(8,128)(2,1)} custom-call(bf16[4,1024,2048]{2,1,0:T(8,128)(2,1)} %green.9, bf16[16,2,64,1024]{3,2,1,0:T(8,128)(2,1)} %refs_0_.1, bf16[4,2,64,1024]{3,2,1,0:T(8,128)(2,1)} %copy-done.4), custom_call_target="tpu_custom_call" | custom-call | flops 4294967296 | bytes 16777216 | tf_op jit(solution)/shard_map/pallas_call | solution.py:203
  16.6 0.0 copy-start.2
  16.6 0.0 copy-start.3
  16.6 7.3 %all-to-all-start.1 = ((bf16[16,2,2,4,16,256]{5,4,3,2,1,0:T(8,128)(2,1)}), bf16[16,2,2,4,16,256]{5,4,3,2,1,0:T(8,128)(2,1)S(1)}, u32[]{:S(2)}, u32[]{:S(2)}) async-start(bf16[16,2,2,4,16,256]{5,4,3,2,1,0:T(8,128)(2,1)} %bitcast.7), calls=%async_computation.1 | async-start | bytes 4194304 | tf_op jit(solution)/shard_map/all_to_all | solution.py:311
  23.9 4.0 %collective-permute-start.7 = (bf16[4,2,64,1024]{3,2,1,0:T(8,128)(2,1)}, bf16[4,2,64,1024]{3,2,1,0:T(8,128)(2,1)}, u32[]{:S(2)}, u32[]{:S(2)}) collective-permute-start(bf16[4,2,64,1024]{3,2,1,0:T(8,128)(2,1)} %get-tuple-element.16), channel_id=1, source_target_pairs={{0,64},{64,0},{1,65},{65,1},{2,66},{66,2},{3,67},{67,3},{4,68},{68... | collective-permute-start | bytes 3145736 | tf_op jit(solution)/shard_map/ppermute | solution.py:29
  27.8 0.0 collective-permute-start.4
  27.8 2.0 %collective-permute-done.4 = bf16[2,2,64,1024]{3,2,1,0:T(8,128)(2,1)} collective-permute-done((bf16[2,2,64,1024]{3,2,1,0:T(8,128)(2,1)S(1)}, bf16[2,2,64,1024]{3,2,1,0:T(8,128)(2,1)}, u32[]{:S(2)}, u32[]{:S(2)}) %collective-permute-start.4) | collective-permute-done | bytes 524320 | tf_op jit(solution)/shard_map/ppermute | solution.py:29
  29.9 0.1 collective-permute-start.5
  30.0 0.0 collective-permute-start
  30.0 0.5 collective-permute-start.2
  30.5 3.0 %filters.1.shaped = bf16[8,96,512]{2,1,0:T(8,128)(2,1)S(1)} custom-call(f32[8,11]{1,0:T(8,128)S(1)} %copy-done.3, f32[32,768]{1,0:T(8,128)S(1)} %copy-done.2), custom_call_target="tpu_custom_call" | custom-call | flops 2883584 | bytes 2097152 | tf_op jit(solution)/shard_map/filters/pallas_call | solution.py:241
  33.5 0.0 collective-permute-done
  33.5 3.5 %collective-permute-start.1 = (bf16[1,2,64,1024]{3,2,1,0:T(8,128)(2,1)}, bf16[1,2,64,1024]{3,2,1,0:T(8,128)(2,1)}, u32[]{:S(2)}, u32[]{:S(2)}) collective-permute-start(bf16[1,2,64,1024]{3,2,1,0:T(8,128)(2,1)} %collective-permute-done), channel_id=1, source_target_pairs={{0,64},{64,0},{1,65},{65,1},{2,66},{66,2},{3,67},{67,3},{4,68},{68... | collective-permute-start | bytes 786440 | tf_op jit(solution)/shard_map/ppermute | solution.py:29
  37.0 0.1 collective-permute-start.3
  37.1 15.1 %collective-permute-done.7.refs_0_ = bf16[4,2,64,1024]{3,2,1,0:T(8,128)(2,1)} collective-permute-done((bf16[4,2,64,1024]{3,2,1,0:T(8,128)(2,1)}, bf16[4,2,64,1024]{3,2,1,0:T(8,128)(2,1)}, u32[]{:S(2)}, u32[]{:S(2)}) %collective-permute-start.7) | collective-permute-done | bytes 1048608 | tf_op jit(solution)/shard_map/ppermute | solution.py:29
  52.2 7.9 %shard_map.56.refs_1_ = bf16[4,4,2,2,4,16,256]{6,5,4,3,2,1,0:T(8,128)(2,1)} custom-call(bf16[4,1024,2048]{2,1,0:T(8,128)(2,1)} %green.9, bf16[4,2,64,1024]{3,2,1,0:T(8,128)(2,1)} %collective-permute-done.7.refs_0_), custom_call_target="tpu_custom_call" | custom-call | flops 2147483648 | bytes 16777216 | tf_op jit(solution)/shard_map/pallas_call | solution.py:203
  60.0 3.4 %collective-permute-done.5.refs_0_ = bf16[2,2,64,1024]{3,2,1,0:T(8,128)(2,1)} collective-permute-done((bf16[2,2,64,1024]{3,2,1,0:T(8,128)(2,1)}, bf16[2,2,64,1024]{3,2,1,0:T(8,128)(2,1)}, u32[]{:S(2)}, u32[]{:S(2)}) %collective-permute-start.5) | collective-permute-done | bytes 524320 | tf_op jit(solution)/shard_map/ppermute | solution.py:29
  63.4 5.1 %shard_map.57.refs_1_ = bf16[4,4,2,2,4,16,256]{6,5,4,3,2,1,0:T(8,128)(2,1)} custom-call(bf16[4,1024,2048]{2,1,0:T(8,128)(2,1)} %green.9, bf16[2,2,64,1024]{3,2,1,0:T(8,128)(2,1)} %collective-permute-done.5.refs_0_, bf16[4,4,2,2,4,16,256]{6,5,4,3,2,1,0:T(8,128)(2,1)} %shard_map.56.refs_1_), custom_call_target="tpu_custom_call", output_to_operand_aliasing={{}: (2, {})} | custom-call | flops 1073741824 | bytes 8388608 | tf_op jit(solution)/shard_map/pallas_call | solution.py:203
  68.5 5.3 %collective-permute-done.3.refs_0_ = bf16[1,2,64,1024]{3,2,1,0:T(8,128)(2,1)} collective-permute-done((bf16[1,2,64,1024]{3,2,1,0:T(8,128)(2,1)}, bf16[1,2,64,1024]{3,2,1,0:T(8,128)(2,1)}, u32[]{:S(2)}, u32[]{:S(2)}) %collective-permute-start.3) | collective-permute-done | bytes 262176 | tf_op jit(solution)/shard_map/ppermute | solution.py:29
  73.8 3.7 %shard_map.58.refs_1_ = bf16[4,4,2,2,4,16,256]{6,5,4,3,2,1,0:T(8,128)(2,1)} custom-call(bf16[4,1024,2048]{2,1,0:T(8,128)(2,1)} %green.9, bf16[1,2,64,1024]{3,2,1,0:T(8,128)(2,1)} %collective-permute-done.3.refs_0_, bf16[4,4,2,2,4,16,256]{6,5,4,3,2,1,0:T(8,128)(2,1)} %shard_map.57.refs_1_), custom_call_target="tpu_custom_call", output_to_operand_aliasing={{}: (2, {})} | custom-call | flops 536870912 | bytes 4194304 | tf_op jit(solution)/shard_map/pallas_call | solution.py:203
  77.5 3.7 %shard_map.59 = bf16[4,4,2,2,4,16,256]{6,5,4,3,2,1,0:T(8,128)(2,1)} custom-call(bf16[4,1024,2048]{2,1,0:T(8,128)(2,1)} %green.9, bf16[1,2,64,1024]{3,2,1,0:T(8,128)(2,1)} %collective-permute-done.1.refs_0_, bf16[4,4,2,2,4,16,256]{6,5,4,3,2,1,0:T(8,128)(2,1)} %shard_map.58.refs_1_), custom_call_target="tpu_custom_call", output_to_operand_aliasing={{}: (2, {})} | custom-call | flops 536870912 | bytes 4194304 | tf_op jit(solution)/shard_map/pallas_call | solution.py:203
  81.3 6.9 %all-to-all-start = ((bf16[16,2,2,4,16,256]{5,4,3,2,1,0:T(8,128)(2,1)}), bf16[16,2,2,4,16,256]{5,4,3,2,1,0:T(8,128)(2,1)}, u32[]{:S(2)}, u32[]{:S(2)}) async-start(bf16[16,2,2,4,16,256]{5,4,3,2,1,0:T(8,128)(2,1)} %bitcast.6), calls=%async_computation | async-start | bytes 4194304 | tf_op jit(solution)/shard_map/all_to_all | solution.py:311
  88.2 2.5 %sums.2.refs_0_ = f32[4,2,4,16,256]{4,3,2,1,0:T(8,128)S(1)} custom-call(bf16[16,2,2,4,16,256]{5,4,3,2,1,0:T(8,128)(2,1)S(1)} %all-to-all-done.1.code), custom_call_target="tpu_custom_call" | custom-call | flops 12582912 | bytes 3145728 | tf_op jit(solution)/shard_map/sums/pallas_call | solution.py:90
  90.7 0.8 copy-done.1
  91.5 25.6 %all-to-all-done.code = bf16[16,2,2,4,16,256]{5,4,3,2,1,0:T(8,128)(2,1)} async-done(((bf16[16,2,2,4,16,256]{5,4,3,2,1,0:T(8,128)(2,1)}), bf16[16,2,2,4,16,256]{5,4,3,2,1,0:T(8,128)(2,1)}, u32[]{:S(2)}, u32[]{:S(2)}) %all-to-all-start) | async-done | bytes 2097184 | tf_op jit(solution)/shard_map/all_to_all | solution.py:311
  117.2 3.7 %sums.3 = f32[4,2,4,16,256]{4,3,2,1,0:T(8,128)} custom-call(bf16[16,2,2,4,16,256]{5,4,3,2,1,0:T(8,128)(2,1)} %all-to-all-done.code, f32[4,2,4,16,256]{4,3,2,1,0:T(8,128)} %copy-done.1), custom_call_target="tpu_custom_call", output_to_operand_aliasing={{}: (1, {})} | custom-call | flops 12582912 | bytes 3145728 | tf_op jit(solution)/shard_map/sums/pallas_call | solution.py:90
  120.9 16.6 %all_to_all.15 = f32[32,16,256]{2,1,0:T(8,128)S(1)} all-to-all(f32[32,16,256]{2,1,0:T(8,128)} %bitcast.5), channel_id=1, replica_groups=mesh['freq_0'=2,'freq_1'=2,'pos_0'=4,'pos_1'=4,'pos_2'=2] {'pos_0','pos_..., dimensions={0} | all-to-all | bytes 1048576 | tf_op jit(solution)/shard_map/all_to_all | solution.py:324
  137.4 2.6 %subtract.1 = bf16[8,256,512]{2,1,0:T(8,128)(2,1)} custom-call(f32[4,2,8,8,256]{4,3,2,1,0:T(8,128)S(1)} %bitcast.4, bf16[8,96,512]{2,1,0:T(8,128)(2,1)S(1)} %filters.1.shaped, bf16[8,256,512]{2,1,0:T(8,128)(2,1)S(1)} %copy-done), custom_call_target="tpu_custom_call" | custom-call | tf_op jit(solution)/shard_map/subtract/pallas_call | solution.py:276
  (11 shorter events, 0.0 us)
Async XLA Ops:
  3.5 3.0 %collective-permute-start.6 = (bf16[4,2,64,1024]{3,2,1,0:T(8,128)(2,1)}, bf16[4,2,64,1024]{3,2,1,0:T(8,128)(2,1)S(1)}, u32[]{:S(2)}, u32[]{:S(2)}) collective-permute-start(bf16[4,2,64,1024]{3,2,1,0:T(8,128)(2,1)} %get-tuple-element.15), channel_id=1, source_target_pairs={{0,32},{32,0},{1,33},{33,1},{2,34},{34,2},{3,35},{35,3},{4,36},{36... | collective-permute-start | bytes 3145736 | tf_op jit(solution)/shard_map/ppermute | solution.py:29
  6.5 1.0 copy-start.4
  16.5 11.3 %copy-start.5 = (bf16[2,2,64,1024]{3,2,1,0:T(8,128)(2,1)S(1)}, bf16[2,2,64,1024]{3,2,1,0:T(8,128)(2,1)}, u32[]{:S(2)}) copy-start(bf16[2,2,64,1024]{3,2,1,0:T(8,128)(2,1)} %get-tuple-element.14) | copy-start | bytes 1572868
  16.6 13.9 %copy-start.2 = (f32[32,768]{1,0:T(8,128)S(1)}, f32[32,768]{1,0:T(8,128)}, u32[]{:S(2)}) copy-start(f32[32,768]{1,0:T(8,128)} %constant.2.clone.table) | copy-start | bytes 294916
  16.6 13.9 %copy-start.3 = (f32[8,11]{1,0:T(8,128)S(1)}, f32[8,11]{1,0:T(8,128)}, u32[]{:S(2)}) copy-start(f32[8,11]{1,0:T(8,128)} %taps.1) | copy-start | bytes 1060
  16.6 64.7 %all-to-all-start.1 = ((bf16[16,2,2,4,16,256]{5,4,3,2,1,0:T(8,128)(2,1)}), bf16[16,2,2,4,16,256]{5,4,3,2,1,0:T(8,128)(2,1)S(1)}, u32[]{:S(2)}, u32[]{:S(2)}) async-start(bf16[16,2,2,4,16,256]{5,4,3,2,1,0:T(8,128)(2,1)} %bitcast.7), calls=%async_computation.1 | async-start | bytes 4194304 | tf_op jit(solution)/shard_map/all_to_all | solution.py:311
  23.9 28.3 %collective-permute-start.7 = (bf16[4,2,64,1024]{3,2,1,0:T(8,128)(2,1)}, bf16[4,2,64,1024]{3,2,1,0:T(8,128)(2,1)}, u32[]{:S(2)}, u32[]{:S(2)}) collective-permute-start(bf16[4,2,64,1024]{3,2,1,0:T(8,128)(2,1)} %get-tuple-element.16), channel_id=1, source_target_pairs={{0,64},{64,0},{1,65},{65,1},{2,66},{66,2},{3,67},{67,3},{4,68},{68... | collective-permute-start | bytes 3145736 | tf_op jit(solution)/shard_map/ppermute | solution.py:29
  27.8 2.0 %collective-permute-start.4 = (bf16[2,2,64,1024]{3,2,1,0:T(8,128)(2,1)S(1)}, bf16[2,2,64,1024]{3,2,1,0:T(8,128)(2,1)}, u32[]{:S(2)}, u32[]{:S(2)}) collective-permute-start(bf16[2,2,64,1024]{3,2,1,0:T(8,128)(2,1)S(1)} %copy-done.5), channel_id=1, source_target_pairs={{0,32},{32,0},{1,33},{33,1},{2,34},{34,2},{3,35},{35,3},{4,36},{36... | collective-permute-start | bytes 1572872 | tf_op jit(solution)/shard_map/ppermute | solution.py:29
  29.9 33.5 %collective-permute-start.5 = (bf16[2,2,64,1024]{3,2,1,0:T(8,128)(2,1)}, bf16[2,2,64,1024]{3,2,1,0:T(8,128)(2,1)}, u32[]{:S(2)}, u32[]{:S(2)}) collective-permute-start(bf16[2,2,64,1024]{3,2,1,0:T(8,128)(2,1)} %collective-permute-done.4), channel_id=1, source_target_pairs={{0,64},{64,0},{1,65},{65,1},{2,66},{66,2},{3,67},{67,3},{4,68},{68... | collective-permute-start | bytes 1572872 | tf_op jit(solution)/shard_map/ppermute | solution.py:29
  30.0 3.5 %collective-permute-start = (bf16[1,2,64,1024]{3,2,1,0:T(8,128)(2,1)}, bf16[1,2,64,1024]{3,2,1,0:T(8,128)(2,1)}, u32[]{:S(2)}, u32[]{:S(2)}) collective-permute-start(bf16[1,2,64,1024]{3,2,1,0:T(8,128)(2,1)} %get-tuple-element.12), channel_id=1, source_target_pairs={{0,32},{32,0},{1,33},{33,1},{2,34},{34,2},{3,35},{35,3},{4,36},{36... | collective-permute-start | bytes 786440 | tf_op jit(solution)/shard_map/ppermute | solution.py:29
  30.0 7.0 %collective-permute-start.2 = (bf16[1,2,64,1024]{3,2,1,0:T(8,128)(2,1)}, bf16[1,2,64,1024]{3,2,1,0:T(8,128)(2,1)}, u32[]{:S(2)}, u32[]{:S(2)}) collective-permute-start(bf16[1,2,64,1024]{3,2,1,0:T(8,128)(2,1)} %get-tuple-element.13), channel_id=1, source_target_pairs={{0,32},{32,0},{1,33},{33,1},{2,34},{34,2},{3,35},{35,3},{4,36},{36... | collective-permute-start | bytes 786440 | tf_op jit(solution)/shard_map/ppermute | solution.py:29
  33.5 44.0 %collective-permute-start.1 = (bf16[1,2,64,1024]{3,2,1,0:T(8,128)(2,1)}, bf16[1,2,64,1024]{3,2,1,0:T(8,128)(2,1)}, u32[]{:S(2)}, u32[]{:S(2)}) collective-permute-start(bf16[1,2,64,1024]{3,2,1,0:T(8,128)(2,1)} %collective-permute-done), channel_id=1, source_target_pairs={{0,64},{64,0},{1,65},{65,1},{2,66},{66,2},{3,67},{67,3},{4,68},{68... | collective-permute-start | bytes 786440 | tf_op jit(solution)/shard_map/ppermute | solution.py:29
  37.0 36.8 %collective-permute-start.3 = (bf16[1,2,64,1024]{3,2,1,0:T(8,128)(2,1)}, bf16[1,2,64,1024]{3,2,1,0:T(8,128)(2,1)}, u32[]{:S(2)}, u32[]{:S(2)}) collective-permute-start(bf16[1,2,64,1024]{3,2,1,0:T(8,128)(2,1)} %collective-permute-done.2), channel_id=1, source_target_pairs={{0,64},{64,0},{1,65},{65,1},{2,66},{66,2},{3,67},{67,3},{4,68},{68... | collective-permute-start | bytes 786440 | tf_op jit(solution)/shard_map/ppermute | solution.py:29
  81.3 35.9 %all-to-all-start = ((bf16[16,2,2,4,16,256]{5,4,3,2,1,0:T(8,128)(2,1)}), bf16[16,2,2,4,16,256]{5,4,3,2,1,0:T(8,128)(2,1)}, u32[]{:S(2)}, u32[]{:S(2)}) async-start(bf16[16,2,2,4,16,256]{5,4,3,2,1,0:T(8,128)(2,1)} %bitcast.6), calls=%async_computation | async-start | bytes 4194304 | tf_op jit(solution)/shard_map/all_to_all | solution.py:311
  90.7 0.8 copy-start.1
  91.5 45.9 %copy-start = (bf16[8,256,512]{2,1,0:T(8,128)(2,1)S(1)}, bf16[8,256,512]{2,1,0:T(8,128)(2,1)}, u32[]{:S(2)}) copy-start(bf16[8,256,512]{2,1,0:T(8,128)(2,1)} %recorded.1) | copy-start | bytes 6291460
